TPU v7x, 512 devices: a whole 4x8x8 slice. The times are simulated.
512 devices in a mesh: ep: 128 (over y, z, core), dp: 4 (over x).
Axes of the slice: x: 4, y: 8, z: 8, core: 2. Of those that a mesh axis runs over, the one named last changes fastest.
Arguments:
- activations: float32 [256, 256, 768], P('ep', 'dp'), may hold values from -6 to 6
- out_grads: float32 [256, 256, 512], P('ep', 'dp'), may hold values from -6 to 6
- counts: int32 [256, 4], P('ep', 'dp'), may hold values from 1 to 64
- slot_weights: float32 [256, 768, 512], P('ep', None, 'dp'), may hold values from -0.21875 to 0.21875
- master: float32 [128, 768, 512], P(None, 'ep', 'dp'), may hold values from -0.21875 to 0.21875
- moment_one: float32 [128, 768, 512], P(None, 'ep', 'dp'), may hold values from -6 to 6
- moment_two: float32 [128, 768, 512], P(None, 'ep', 'dp'), may hold values from 1 to 100
- old_table: int32 [256, 1], replicated, may hold values from 0 to 127
- new_table: int32 [256, 1], replicated, may hold values from 0 to 127
Outputs:
- outputs: float32 [256, 256, 512], P('ep', 'dp')
- input_grads: float32 [256, 256, 768], P('ep', 'dp')
- new_master: float32 [128, 768, 512], P(None, 'ep', 'dp')
- new_moment_one: float32 [128, 768, 512], P(None, 'ep', 'dp')
- new_moment_two: float32 [128, 768, 512], P(None, 'ep', 'dp')
- new_slots: float32 [256, 768, 512], P('ep', None, 'dp')
Inputs may be any that keep to these rules, and one draw needn't show every extreme that they name: `old_table`: every expert is named by at least one old slot. `new_table`: every expert is named by at least one new slot.
All inputs are finite; a program needn't handle non-finite values.
Results may differ from a plain program's by a relative error of at most 0.00007.
Values sent between devices are 32-bit elements; how exact they have to be, the bound alone decides.
No kernel may reach another device: no remote copies, remote signals or barrier semaphores. Data moves between devices by JAX's collectives and lax.ppermute only.
A program may use at most 64 MiB of HBM per device.

v0:
```python
import jax
import jax.numpy as jnp
from jax import lax
from jax.sharding import PartitionSpec as P

STEP = 100
beta_one = 0.9
beta_two = 0.999
learn_rate = 0.02
epsilon = 1e-08
decay_rate = 0.1


def adamw(master, moment_one, moment_two, expert_grad):
    first_new = beta_one * moment_one + (1.0 - beta_one) * expert_grad
    second_new = beta_two * moment_two + (1.0 - beta_two) * expert_grad * expert_grad
    first_hat = first_new / (1.0 - beta_one**STEP)
    second_hat = second_new / (1.0 - beta_two**STEP)
    updated = master - learn_rate * (
        first_hat / (jnp.sqrt(second_hat) + epsilon) + decay_rate * master
    )
    return (updated, first_new, second_new)


def local(
    activations,
    out_grads,
    counts,
    slot_weights,
    master,
    moment_one,
    moment_two,
    old_table,
    new_table,
):
    precise = lax.Precision.HIGHEST
    experts_ids = jnp.arange(master.shape[0], dtype=jnp.int32)
    old_onehot = (old_table[:, 0][None, :] == experts_ids[:, None]).astype(jnp.float32)
    positions = jnp.arange(activations.shape[1], dtype=jnp.int32)
    live_rows = (positions[None, :] < counts).astype(jnp.float32)
    masked_acts = activations * live_rows[:, :, None]
    masked_grads = out_grads * live_rows[:, :, None]
    whole_weights = lax.all_gather(slot_weights, "dp", axis=2, tiled=True)
    outputs = jnp.einsum("srf,sfd->srd", masked_acts, whole_weights, precision=precise)
    input_grads = jnp.einsum("srd,sfd->srf", masked_grads, whole_weights, precision=precise)
    every_act = lax.all_gather(masked_acts, "dp", axis=1, tiled=True)
    own_columns = lax.all_to_all(masked_grads, "dp", split_axis=2, concat_axis=1, tiled=True)
    column_grad = jnp.einsum("srf,srd->sfd", every_act, own_columns, precision=precise)
    arrived = lax.all_to_all(column_grad, "ep", split_axis=1, concat_axis=0, tiled=True)
    expert_grad = jnp.einsum("es,sfd->efd", old_onehot, arrived, precision=precise)
    new_master, new_moment_one, new_moment_two = adamw(master, moment_one, moment_two, expert_grad)
    new_onehot = (new_table[:, 0][:, None] == experts_ids[None, :]).astype(jnp.float32)
    picked = jnp.einsum("se,efd->sfd", new_onehot, new_master, precision=precise)
    new_slots = lax.all_to_all(picked, "ep", split_axis=0, concat_axis=1, tiled=True)
    return (outputs, input_grads, new_master, new_moment_one, new_moment_two, new_slots)


def solution(mesh):
    in_specs = (
        P("ep", "dp", None),
        P("ep", "dp", None),
        P("ep", "dp"),
        P("ep", None, "dp"),
        P(None, "ep", "dp"),
        P(None, "ep", "dp"),
        P(None, "ep", "dp"),
        P(),
        P(),
    )
    out_specs = (
        P("ep", "dp", None),
        P("ep", "dp", None),
        P(None, "ep", "dp"),
        P(None, "ep", "dp"),
        P(None, "ep", "dp"),
        P("ep", None, "dp"),
    )
    return jax.shard_map(local, mesh=mesh, in_specs=in_specs, out_specs=out_specs, check_vma=False)
```

profile of v0, /device:TPU:8, one launch (start us, length us, event | category | flops | bytes accessed | tf_op | source)
XLA Modules:
  0.0 141.4 jit_solution(7682760392878343886)
XLA Ops:
  7.2 0.0 all-gather.5.cloned.1.call-start
  7.2 0.7 compare_convert_fusion
  7.9 1.8 %broadcast_multiply_fusion = f32[2,64,768]{2,1,0:T(8,128)} fusion(f32[2,64,768]{2,1,0:T(8,128)} %param.9, f32[2,64]{1,0:T(2,128)S(1)} %compare_convert_fusion), kind=kLoop, calls=%fused_computation.4 | loop fusion | flops 98304 | bytes 786944 | tf_op jit(solution)/shard_map/mul | solution.py:41
  9.8 0.0 all-gather.5.cloned.1.call-update
  9.8 0.0 all-gather.3.cloned.1.call-start
  9.8 0.7 all-gather.3.cloned.1.call-update
  10.5 1.0 broadcast_multiply_fusion.1
  11.6 0.2 copy.31
  11.8 0.6 reshape.38
  12.4 10.8 %all_to_all.54 = f32[4,1,16384]{2,1,0:T(1,128)S(1)} all-to-all(f32[4,1,16384]{2,1,0:T(1,128)S(1)} %reshape.38), channel_id=1, replica_groups=mesh['ep'=128,'dp'=4] {'dp'}, dimensions={0} | all-to-all | bytes 524288 | tf_op jit(solution)/shard_map/all_to_all | solution.py:47
  23.2 0.5 broadcast.23
  23.7 1.4 reduce
  25.1 0.4 reshape.39
  25.5 0.2 copy.32
  25.7 21.4 %all-gather.5.cloned.1.call-done = f32[2,256,768]{2,1,0:T(8,128)} async-done(((f32[2,64,768]{2,1,0:T(8,128)}), f32[2,256,768]{2,1,0:T(8,128)}) %all-gather.5.cloned.1.call-update) | async-done | bytes 1572880 | tf_op jit(solution)/shard_map/all_gather | solution.py:46
  47.1 4.1 %fusion.12 = f32[2,768,128]{2,1,0:T(8,128)S(1)} fusion(f32[2,256,768]{2,1,0:T(8,128)} %all-gather.5.cloned.1.call-done, f32[2,256,128]{2,1,0:T(8,128)S(1)} %bitcast.39), kind=kOutput, calls=%fused_computation.17 | convolution fusion | flops 603979776 | bytes 2621440 | tf_op jit(solution)/shard_map/srf,srd->sfd/dot_general | solution.py:48
  51.3 0.6 copy.33
  51.9 0.0 copy-start.7
  51.9 39.8 %all_to_all.55 = f32[2,768,128]{2,0,1:T(2,128)S(1)} all-to-all(f32[2,768,128]{2,0,1:T(2,128)S(1)} %copy.33), channel_id=1, replica_groups=mesh['ep'=128,'dp'=4] {'ep'}, dimensions={1} | all-to-all | bytes 1572864 | tf_op jit(solution)/shard_map/all_to_all | solution.py:49
  91.7 0.3 copy.34
  92.0 0.0 copy-done.3
  92.0 0.0 copy-done.4
  92.0 1.5 %multiply_subtract_fusion = (f32[128,6,128]{2,0,1:T(8,128)S(1)}, f32[128,6,128]{2,0,1:T(8,128)}, f32[128,6,128]{2,0,1:T(8,128)}) fusion(f32[128,6,128]{2,0,1:T(8,128)S(1)} %copy-done.3, f32[128,6,128]{2,0,1:T(8,128)S(1)} %copy-done.4, f32[128,6,128]{2,0,1:T(8,128)S(1)} %copy-done.5, f32[256,6,128]{2,0,1:T(8,128)S(1)} %bitcast.36, s32[256]{0:T(256)S(1)} %bitcast.40), kind=kOutput, calls=%fused_computation.2 | convolution fusion | flops 303497216 | bytes 3146752 | tf_op jit(solution)/shard_map/es,sfd->efd/dot_general | solution.py:50
  93.6 0.5 fusion.5
  94.1 1.5 %copy.35 = f32[256,6,128]{2,1,0:T(8,128)} copy(f32[256,6,128]{2,0,1:T(8,128)S(1)} %fusion.5) | data formatting | bytes 1572864 | tf_op jit(solution)/shard_map/se,efd->sfd/dot_general | solution.py:53
  95.6 6.2 %all-to-all-start.2 = ((f32[256,6,128]{2,1,0:T(8,128)}), f32[256,6,128]{2,1,0:T(8,128)S(1)}, u32[]{:S(2)}, u32[]{:S(2)}) async-start(f32[256,6,128]{2,1,0:T(8,128)} %copy.35), calls=%async_computation.2 | async-start | bytes 2097152 | tf_op jit(solution)/shard_map/all_to_all | solution.py:54
  101.8 0.0 all-gather.3.cloned.1.call-done
  101.8 4.8 %fusion.10 = f32[2,64,512]{2,1,0:T(8,128)} fusion(f32[2,64,768]{2,1,0:T(8,128)S(1)} %copy-done.1, f32[2,768,512]{2,1,0:T(8,128)} %all-gather.3.cloned.1.call-done), kind=kOutput, calls=%fused_computation.15 | convolution fusion | flops 603979776 | bytes 3801088 | tf_op jit(solution)/shard_map/srf,sfd->srd/dot_general | solution.py:44
  106.6 3.9 %fusion.11 = f32[2,64,768]{2,1,0:T(8,128)} fusion(f32[2,64,512]{2,1,0:T(8,128)S(1)} %broadcast_multiply_fusion.1, f32[2,768,512]{2,1,0:T(8,128)S(1)} %copy-done), kind=kOutput, calls=%fused_computation.16 | convolution fusion | flops 603979776 | bytes 3801088 | tf_op jit(solution)/shard_map/srd,sfd->srf/dot_general | solution.py:45
  110.5 22.7 %all-to-all-done.2 = f32[256,6,128]{2,1,0:T(8,128)S(1)} async-done(((f32[256,6,128]{2,1,0:T(8,128)}), f32[256,6,128]{2,1,0:T(8,128)S(1)}, u32[]{:S(2)}, u32[]{:S(2)}) %all-to-all-start.2) | async-done | bytes 786464 | tf_op jit(solution)/shard_map/all_to_all | solution.py:54
  133.2 0.4 copy.36
  133.6 0.9 copy.37
  (13 shorter events, 0.0 us)
Async XLA Ops:
  7.2 40.0 %all-gather.5.cloned.1.call-start = ((), (), s32[]{:S(2)}) async-start(), calls=%async_computation.4 | async-start | bytes 1966080 | tf_op jit(solution)/shard_map/all_gather | solution.py:46
  9.8 92.0 %all-gather.3.cloned.1.call-start = ((), (), s32[]{:S(2)}) async-start(), calls=%async_computation.3 | async-start | bytes 3932160 | tf_op jit(solution)/shard_map/all_gather | solution.py:43
  47.1 44.9 %copy-start.3 = (f32[128,6,128]{2,0,1:T(8,128)S(1)}, f32[128,6,128]{2,0,1:T(8,128)}, u32[]{:S(2)}) copy-start(f32[128,6,128]{2,0,1:T(8,128)} %param.13) | copy-start | bytes 1179652
  47.1 44.9 %copy-start.4 = (f32[128,6,128]{2,0,1:T(8,128)S(1)}, f32[128,6,128]{2,0,1:T(8,128)}, u32[]{:S(2)}) copy-start(f32[128,6,128]{2,0,1:T(8,128)} %param.14) | copy-start | bytes 1179652
  47.1 44.9 %copy-start.5 = (f32[128,6,128]{2,0,1:T(8,128)S(1)}, f32[128,6,128]{2,0,1:T(8,128)}, u32[]{:S(2)}) copy-start(f32[128,6,128]{2,0,1:T(8,128)} %param.15) | copy-start | bytes 1179652
  47.1 44.9 %copy-start.6 = (s32[256,1]{0,1:T(1,128)S(1)}, s32[256,1]{0,1:T(1,128)}, u32[]{:S(2)}) copy-start(s32[256,1]{0,1:T(1,128)} %param.16) | copy-start | bytes 3076
  51.9 41.7 %copy-start.7 = (s32[256,1]{0,1:T(1,128)S(1)}, s32[256,1]{0,1:T(1,128)}, u32[]{:S(2)}) copy-start(s32[256,1]{0,1:T(1,128)} %param.17) | copy-start | bytes 3076
  93.6 13.0 %copy-start.2 = (f32[128,6,128]{2,0,1:T(8,128)}, f32[128,6,128]{2,0,1:T(8,128)S(1)}, u32[]{:S(2)}) copy-start(f32[128,6,128]{2,0,1:T(8,128)S(1)} %get-tuple-element.24) | copy-start | bytes 1179652
  93.6 8.2 %copy-start.1 = (f32[2,64,768]{2,1,0:T(8,128)S(1)}, f32[2,64,768]{2,1,0:T(8,128)}, u32[]{:S(2)}) copy-start(f32[2,64,768]{2,1,0:T(8,128)} %broadcast_multiply_fusion) | copy-start | bytes 1179652
  95.6 37.6 %all-to-all-start.2 = ((f32[256,6,128]{2,1,0:T(8,128)}), f32[256,6,128]{2,1,0:T(8,128)S(1)}, u32[]{:S(2)}, u32[]{:S(2)}) async-start(f32[256,6,128]{2,1,0:T(8,128)} %copy.35), calls=%async_computation.2 | async-start | bytes 2097152 | tf_op jit(solution)/shard_map/all_to_all | solution.py:54
  101.8 4.8 %copy-start = (f32[2,768,512]{2,1,0:T(8,128)S(1)}, f32[2,768,512]{2,1,0:T(8,128)}, u32[]{:S(2)}) copy-start(f32[2,768,512]{2,1,0:T(8,128)} %all-gather.3.cloned.1.call-done) | copy-start | bytes 9437188
Sparse Core Ops, SparseCore 0:
  10.7 36.4 all-gather.4
  49.2 48.6 all-gather.2
where the time goes:
time: 142 us; the launch traced here: 141 us
  blocking collectives  50.6 us (36%)
  waiting for transfers between devices  44.9 us (32%)
  matrix products  14.8 us (10%)
  between operations  14.2 us (10%)
  starting transfers between devices  6.29 us (4%)
  local copies, waits for them, and re-layouts  5.63 us (4%)
  other arithmetic  4.96 us (3%)
    all_to_all x1, blocking collectives, local(): lax.all_to_all(column_grad, 'ep', split_axis=1, concat_axis=0, tiled=True)  39.8 us
    all_to_all x1, waiting for transfers between devices, local(): lax.all_to_all(picked, 'ep', split_axis=0, concat_axis=1, tiled=True)  22.7 us
    all_gather x1, waiting for transfers between devices, local(): every_act = lax.all_gather(masked_acts, 'dp', axis=1, tiled=True)  21.4 us
    all_to_all x1, blocking collectives, local(): lax.all_to_all(masked_grads, 'dp', split_axis=2, concat_axis=1, tiled=True)  10.8 us
    all_to_all x1, starting transfers between devices, local(): lax.all_to_all(picked, 'ep', split_axis=0, concat_axis=1, tiled=True)  6.21 us
    dot_general x1, matrix products, local(): jnp.einsum('srf,sfd->srd', masked_acts, whole_weights, precision=precise)  4.76 us
    dot_general x1, matrix products, local(): jnp.einsum('srf,srd->sfd', every_act, own_columns, precision=precise)  4.13 us
    dot_general x1, matrix products, local(): jnp.einsum('srd,sfd->srf', masked_grads, whole_weights, precision=precise)  3.89 us
  transfers between devices with their start and end apart: 3, of which 2 were waited for; matrix products, arithmetic and copies ran while one was open for 15% of the time, Pallas kernels for 0%

commit v1 on v0

--- a/solution.py
+++ b/solution.py
@@ -43,7 +43,9 @@
     whole_weights = lax.all_gather(slot_weights, "dp", axis=2, tiled=True)
     outputs = jnp.einsum("srf,sfd->srd", masked_acts, whole_weights, precision=precise)
     input_grads = jnp.einsum("srd,sfd->srf", masked_grads, whole_weights, precision=precise)
-    every_act = lax.all_gather(masked_acts, "dp", axis=1, tiled=True)
+    every_act = jnp.concatenate(
+        lax.all_to_all(jnp.stack([masked_acts] * lax.axis_size("dp")), "dp", 0, 0), axis=1
+    )
     own_columns = lax.all_to_all(masked_grads, "dp", split_axis=2, concat_axis=1, tiled=True)
     column_grad = jnp.einsum("srf,srd->sfd", every_act, own_columns, precision=precise)
     arrived = lax.all_to_all(column_grad, "ep", split_axis=1, concat_axis=0, tiled=True)

time: 142 us -> 150 us (1.056)
  the two profiles are of different devices: /device:TPU:8 before, /device:TPU:1 now
where the time goes in v1:
time: 150 us; the launch traced here: 149 us
  blocking collectives  86.5 us (58%)
  waiting for transfers between devices  15.7 us (10%)
  between operations  14.2 us (9%)
  matrix products  13.3 us (9%)
  starting transfers between devices  8.44 us (6%)
  local copies, waits for them, and re-layouts  6.74 us (4%)
  other arithmetic  4.21 us (3%)
    all_to_all x1, blocking collectives, local(): lax.all_to_all(column_grad, 'ep', split_axis=1, concat_axis=0, tiled=True)  49.7 us
    all_to_all x1, blocking collectives, local(): lax.all_to_all(picked, 'ep', split_axis=0, concat_axis=1, tiled=True)  36.8 us
    all_to_all x1, waiting for transfers between devices, local(): lax.all_to_all(jnp.stack([masked_acts] * lax.axis_size('dp')), 'dp', 0, 0)  10.6 us
    all_to_all x1, starting transfers between devices, local(): lax.all_to_all(masked_grads, 'dp', split_axis=2, concat_axis=1, tiled=True)  4.84 us
    dot_general x1, matrix products, local(): jnp.einsum('srf,sfd->srd', masked_acts, whole_weights, precision=precise)  4.76 us
    all_to_all x1, waiting for transfers between devices, local(): lax.all_to_all(masked_grads, 'dp', split_axis=2, concat_axis=1, tiled=True)  4.44 us
    dot_general x1, matrix products, local(): jnp.einsum('srd,sfd->srf', masked_grads, whole_weights, precision=precise)  3.9 us
    all_to_all x1, starting transfers between devices, local(): lax.all_to_all(jnp.stack([masked_acts] * lax.axis_size('dp')), 'dp', 0, 0)  3.56 us
  transfers between devices with their start and end apart: 3, of which 2 were waited for; matrix products, arithmetic and copies ran while one was open for 7% of the time, Pallas kernels for 0%

profile of v1, /device:TPU:1, one launch (start us, length us, event | category | flops | bytes accessed | tf_op | source)
XLA Modules:
  0.0 149.1 jit_solution(11483834138764441623)
XLA Ops:
  7.2 0.7 compare_convert_fusion
  7.9 1.0 broadcast_multiply_fusion.1
  8.9 0.2 copy.36
  9.2 1.3 reshape.48
  10.4 4.8 %all-to-all-start.1 = ((f32[4,1,16384]{2,1,0:T(1,128)}), f32[4,1,16384]{2,1,0:T(1,128)S(1)}, u32[]{:S(2)}, u32[]{:S(2)}) async-start(f32[4,1,16384]{2,1,0:T(1,128)} %reshape.48), calls=%async_computation.1 | async-start | bytes 524288 | tf_op jit(solution)/shard_map/all_to_all | solution.py:49
  15.3 1.1 broadcast_multiply_fusion
  16.4 4.4 %all-to-all-done.1 = f32[4,1,16384]{2,1,0:T(1,128)S(1)} async-done(((f32[4,1,16384]{2,1,0:T(1,128)}), f32[4,1,16384]{2,1,0:T(1,128)S(1)}, u32[]{:S(2)}, u32[]{:S(2)}) %all-to-all-start.1) | async-done | bytes 262176 | tf_op jit(solution)/shard_map/all_to_all | solution.py:49
  20.8 1.3 stack.2
  22.1 3.6 %all-to-all-start = ((f32[4,2,64,768]{3,2,1,0:T(8,128)}), f32[4,2,64,768]{3,2,1,0:T(8,128)S(1)}, u32[]{:S(2)}, u32[]{:S(2)}) async-start(f32[4,2,64,768]{3,2,1,0:T(8,128)} %stack.2), calls=%async_computation | async-start | bytes 3145728 | tf_op jit(solution)/shard_map/all_to_all | solution.py:47
  25.6 0.0 all-gather.2.cloned.1.call-start
  25.7 0.7 all-gather.2.cloned.1.call-update
  26.4 0.5 broadcast.25
  26.9 1.4 reduce
  28.3 0.4 reshape.49
  28.7 0.2 copy.37
  28.9 10.6 %all-to-all-done = f32[4,2,64,768]{3,2,1,0:T(8,128)S(1)} async-done(((f32[4,2,64,768]{3,2,1,0:T(8,128)}), f32[4,2,64,768]{3,2,1,0:T(8,128)S(1)}, u32[]{:S(2)}, u32[]{:S(2)}) %all-to-all-start) | async-done | bytes 1572896 | tf_op jit(solution)/shard_map/all_to_all | solution.py:47
  39.5 0.1 copy.35
  39.6 0.0 copy-start.2
  39.6 0.0 copy-start.4
  39.7 0.0 copy-start.5
  39.7 2.6 %fusion.12 = f32[2,768,128]{2,1,0:T(8,128)S(1)} fusion(f32[2,256,768]{2,1,0:T(8,128)S(1)} %bitcast.36, f32[2,256,128]{2,1,0:T(8,128)S(1)} %bitcast.43), kind=kOutput, calls=%fused_computation.17 | convolution fusion | flops 603979776 | bytes 2621440 | tf_op jit(solution)/shard_map/srf,srd->sfd/dot_general | solution.py:50
  42.3 0.6 copy.39
  42.9 49.7 %all_to_all.59 = f32[2,768,128]{2,0,1:T(2,128)S(1)} all-to-all(f32[2,768,128]{2,0,1:T(2,128)S(1)} %copy.39), channel_id=1, replica_groups=mesh['ep'=128,'dp'=4] {'ep'}, dimensions={1} | all-to-all | bytes 1572864 | tf_op jit(solution)/shard_map/all_to_all | solution.py:51
  92.6 0.3 copy.40
  92.9 1.5 %multiply_subtract_fusion = (f32[128,6,128]{2,0,1:T(8,128)S(1)}, f32[128,6,128]{2,0,1:T(8,128)}, f32[128,6,128]{2,0,1:T(8,128)}) fusion(f32[128,6,128]{2,0,1:T(8,128)S(1)} %copy-done.2, f32[128,6,128]{2,0,1:T(8,128)S(1)} %copy-done.3, f32[128,6,128]{2,0,1:T(8,128)S(1)} %copy-done.4, f32[256,6,128]{2,0,1:T(8,128)S(1)} %bitcast.40, s32[256]{0:T(256)S(1)} %bitcast.44), kind=kOutput, calls=%fused_computation.2 | convolution fusion | flops 303497216 | bytes 3146752 | tf_op jit(solution)/shard_map/es,sfd->efd/dot_general | solution.py:52
  94.5 0.5 fusion.5
  95.0 0.5 copy.41
  95.5 36.8 %all_to_all.60 = f32[256,6,128]{2,1,0:T(8,128)S(1)} all-to-all(f32[256,6,128]{2,1,0:T(8,128)S(1)} %copy.41), channel_id=1, replica_groups=mesh['ep'=128,'dp'=4] {'ep'}, dimensions={0} | all-to-all | bytes 1572864 | tf_op jit(solution)/shard_map/all_to_all | solution.py:56
  132.2 0.4 copy.42
  132.7 0.9 copy.43
  133.6 4.8 %fusion.10 = f32[2,64,512]{2,1,0:T(8,128)} fusion(f32[2,64,768]{2,1,0:T(8,128)S(1)} %broadcast_multiply_fusion, f32[2,768,512]{2,1,0:T(8,128)} %all-gather.2.cloned.1.call-done), kind=kOutput, calls=%fused_computation.15 | convolution fusion | flops 603979776 | bytes 3801088 | tf_op jit(solution)/shard_map/srf,sfd->srd/dot_general | solution.py:44
  138.4 3.9 %fusion.11 = f32[2,64,768]{2,1,0:T(8,128)} fusion(f32[2,64,512]{2,1,0:T(8,128)S(1)} %broadcast_multiply_fusion.1, f32[2,768,512]{2,1,0:T(8,128)S(1)} %copy-done), kind=kOutput, calls=%fused_computation.16 | convolution fusion | flops 603979776 | bytes 3801088 | tf_op jit(solution)/shard_map/srd,sfd->srf/dot_general | solution.py:45
  (12 shorter events, 0.0 us)
Async XLA Ops:
  10.4 10.4 %all-to-all-start.1 = ((f32[4,1,16384]{2,1,0:T(1,128)}), f32[4,1,16384]{2,1,0:T(1,128)S(1)}, u32[]{:S(2)}, u32[]{:S(2)}) async-start(f32[4,1,16384]{2,1,0:T(1,128)} %reshape.48), calls=%async_computation.1 | async-start | bytes 524288 | tf_op jit(solution)/shard_map/all_to_all | solution.py:49
  22.1 17.4 %all-to-all-start = ((f32[4,2,64,768]{3,2,1,0:T(8,128)}), f32[4,2,64,768]{3,2,1,0:T(8,128)S(1)}, u32[]{:S(2)}, u32[]{:S(2)}) async-start(f32[4,2,64,768]{3,2,1,0:T(8,128)} %stack.2), calls=%async_computation | async-start | bytes 3145728 | tf_op jit(solution)/shard_map/all_to_all | solution.py:47
  25.6 107.9 %all-gather.2.cloned.1.call-start = ((), (), s32[]{:S(2)}) async-start(), calls=%async_computation.4 | async-start | bytes 3932160 | tf_op jit(solution)/shard_map/all_gather | solution.py:43
  39.6 53.3 %copy-start.2 = (f32[128,6,128]{2,0,1:T(8,128)S(1)}, f32[128,6,128]{2,0,1:T(8,128)}, u32[]{:S(2)}) copy-start(f32[128,6,128]{2,0,1:T(8,128)} %param.13) | copy-start | bytes 1179652
  39.6 53.2 %copy-start.3 = (f32[128,6,128]{2,0,1:T(8,128)S(1)}, f32[128,6,128]{2,0,1:T(8,128)}, u32[]{:S(2)}) copy-start(f32[128,6,128]{2,0,1:T(8,128)} %param.14) | copy-start | bytes 1179652
  39.6 53.2 %copy-start.4 = (f32[128,6,128]{2,0,1:T(8,128)S(1)}, f32[128,6,128]{2,0,1:T(8,128)}, u32[]{:S(2)}) copy-start(f32[128,6,128]{2,0,1:T(8,128)} %param.15) | copy-start | bytes 1179652
  39.7 53.2 %copy-start.5 = (s32[256,1]{0,1:T(1,128)S(1)}, s32[256,1]{0,1:T(1,128)}, u32[]{:S(2)}) copy-start(s32[256,1]{0,1:T(1,128)} %param.16) | copy-start | bytes 3076
  42.9 51.5 %copy-start.6 = (s32[256,1]{0,1:T(1,128)S(1)}, s32[256,1]{0,1:T(1,128)}, u32[]{:S(2)}) copy-start(s32[256,1]{0,1:T(1,128)} %param.17) | copy-start | bytes 3076
  94.4 38.2 %copy-start.1 = (f32[128,6,128]{2,0,1:T(8,128)}, f32[128,6,128]{2,0,1:T(8,128)S(1)}, u32[]{:S(2)}) copy-start(f32[128,6,128]{2,0,1:T(8,128)S(1)} %get-tuple-element.24) | copy-start | bytes 1179652
  133.6 4.8 %copy-start = (f32[2,768,512]{2,1,0:T(8,128)S(1)}, f32[2,768,512]{2,1,0:T(8,128)}, u32[]{:S(2)}) copy-start(f32[2,768,512]{2,1,0:T(8,128)} %all-gather.2.cloned.1.call-done) | copy-start | bytes 9437188
Sparse Core Ops, SparseCore 0:
  28.6 54.1 all-gather.1
